TPU v7x, 32 devices: a whole 2x2x4 slice. The times are simulated.
32 devices in a mesh: layer: 2 (over core), latent: 16 (over z, y, x).
Axes of the slice: x: 2, y: 2, z: 4, core: 2. Of those that a mesh axis runs over, the one named last changes fastest.
Arguments:
- activations: bfloat16 [2, 512, 2048], P('layer', 'latent'), may hold values from -15 to 15
- enc_weight: bfloat16 [2, 2048, 16384], P('layer', None, 'latent'), may hold values from -0.09375 to 0.09375
- enc_bias: float32 [16384], P('latent'), may hold values from -3 to 3
- dec_weight: bfloat16 [2, 16384, 2048], P('layer', 'latent'), may hold values from -0.1796875 to 0.1796875
- dec_bias: float32 [2, 2048], P('layer'), may hold values from -3 to 3
- active_mask: int32 [512, 16384], P(None, 'latent'), may hold values 0 or 1
Outputs:
- grad_enc: bfloat16 [2, 2048, 16384], P('layer', None, 'latent')
- grad_dec: bfloat16 [2, 16384, 2048], P('layer', 'latent')
- loss_value: float32 [], replicated
All inputs are finite; a program needn't handle non-finite values. No bound on the sum of `active_mask` on one device may be relied on, other than what follows from the above.
Results may differ from a plain program's by a relative error of at most 0.0065.
Values may be sent and summed in bfloat16 or wider, within the bound.
A program may use at most 128 MiB of HBM per device.

v0:
```python
import jax
import jax.numpy as jnp
from jax import lax
from jax.sharding import PartitionSpec as P

sparsity_weight = 0.4


def per_device(activations, enc_weight, enc_bias, dec_weight, dec_bias, active_mask):
    local_rows = activations[0]
    encoder = enc_weight[0]
    decoder = dec_weight[0]
    token_all = lax.all_gather(local_rows, "latent", axis=0, tiled=True)
    layer_pre = jnp.dot(token_all, encoder, preferred_element_type=jnp.float32)
    dec_float = decoder.astype(jnp.float32)
    row_norm = jnp.sqrt(jnp.sum(dec_float * dec_float, axis=1) + 1e-06)
    preact, norm_sum = lax.psum((layer_pre, row_norm), "layer")
    preact = preact + enc_bias
    gating = active_mask.astype(jnp.float32)
    latent_code = preact * gating
    code_b = latent_code.astype(jnp.bfloat16)
    layer_index = lax.axis_index("layer")
    recon_share = (
        lax.psum_scatter(
            jnp.dot(code_b, decoder, preferred_element_type=jnp.float32),
            "latent",
            scatter_dimension=0,
            tiled=True,
        )
        + dec_bias[0]
    )
    error_share = recon_share - local_rows.astype(jnp.float32)
    square_part = 0.5 * jnp.sum(error_share * error_share)
    error_b = lax.all_gather(error_share.astype(jnp.bfloat16), "latent", axis=0, tiled=True)
    layer_grad = jnp.einsum("td,fd->tf", error_b, decoder, preferred_element_type=jnp.float32)
    code_grad = lax.psum(layer_grad, "layer") + sparsity_weight * norm_sum
    preact_grad = (code_grad * gating).astype(jnp.bfloat16)
    grad_enc = jnp.einsum(
        "td,tf->df", token_all, preact_grad, preferred_element_type=jnp.float32
    ).astype(jnp.bfloat16)
    code_total = jnp.sum(latent_code, axis=0)
    shrink = sparsity_weight * code_total[:, None] * dec_float / row_norm[:, None]
    grad_dec = (
        jnp.einsum("tf,td->fd", code_b, error_b, preferred_element_type=jnp.float32) + shrink
    ).astype(jnp.bfloat16)
    sparse_part = jnp.where(
        layer_index == 0, sparsity_weight * jnp.sum(latent_code * norm_sum), 0.0
    )
    loss_total = lax.psum(square_part + sparse_part, ("layer", "latent"))
    loss_value = loss_total / (active_mask.shape[0] * token_all.shape[1])
    return (grad_enc[None], grad_dec[None], loss_value)


def solution(mesh):
    placed = (
        P("layer", "latent", None),
        P("layer", None, "latent"),
        P("latent"),
        P("layer", "latent", None),
        P("layer", None),
        P(None, "latent"),
    )
    return jax.shard_map(
        per_device,
        mesh=mesh,
        in_specs=placed,
        out_specs=(P("layer", None, "latent"), P("layer", "latent", None), P()),
        check_vma=False,
    )
```

profile of v0, /device:TPU:0, one launch (start us, length us, event | category | flops | bytes accessed | tf_op | source)
XLA Modules:
  0.0 342.8 jit_solution(5819471263152638103)
XLA Ops:
  7.2 0.0 all-gather.6.cloned.1.call-start
  7.2 0.7 all-gather.6.cloned.1.call-update
  7.9 0.0 all-reduce.3.cloned.1.call-start
  7.9 65.9 %all-gather.6.cloned.1.call-done = bf16[1,512,2048]{2,1,0:T(8,128)(2,1)} async-done(((bf16[1,32,2048]{2,1,0:T(8,128)(2,1)}), bf16[1,512,2048]{2,1,0:T(8,128)(2,1)}) %all-gather.6.cloned.1.call-update) | async-done | bytes 2097168 | tf_op jit(solution)/shard_map/all_gather | solution.py:13
  73.9 6.5 %fusion.8 = f32[512,1024]{1,0:T(8,128)} fusion(bf16[1,2048,1024]{2,1,0:T(8,128)(2,1)} %param.7, bf16[1,512,2048]{2,1,0:T(8,128)(2,1)} %all-gather.6.cloned.1.call-done), kind=kOutput, calls=%fused_computation.10 | convolution fusion | flops 2147483648 | bytes 8388608 | tf_op jit(solution)/shard_map/dot_general | solution.py:14
  80.4 0.0 all-reduce.3.cloned.1.call-update
  80.4 0.0 reduce-scatter.2.cloned.1.call-start
  80.4 3.2 fusion
  83.7 2.5 psum.30
  86.2 14.5 %all-reduce.3.cloned.1.call-done = f32[512,1024]{1,0:T(8,128)} async-done(((f32[512,1024]{1,0:T(8,128)}), f32[512,1024]{1,0:T(8,128)}) %all-reduce.3.cloned.1.call-update) | async-done | bytes 2097168 | tf_op jit(solution)/shard_map/psum | solution.py:17
  100.6 2.9 multiply_reduce_fusion
  103.6 4.4 %fusion.6 = f32[512,2048]{1,0:T(8,128)} fusion(bf16[1,1024,2048]{2,1,0:T(8,128)(2,1)S(1)} %copy-done, bf16[512,1024]{1,0:T(8,128)(2,1)S(1)} %get-tuple-element.8), kind=kOutput, calls=%fused_computation.8 | convolution fusion | flops 2147483648 | bytes 9437184 | tf_op jit(solution)/shard_map/dot_general | solution.py:25
  107.9 0.0 reduce-scatter.2.cloned.1.call-update
  108.0 0.0 all-gather.4.cloned.1.call-start
  108.0 96.5 %reduce-scatter.2.cloned.1.call-done = f32[32,2048]{1,0:T(8,128)} async-done(((f32[512,2048]{1,0:T(8,128)}), f32[32,2048]{1,0:T(8,128)}) %reduce-scatter.2.cloned.1.call-update) | async-done | bytes 262160 | tf_op jit(solution)/shard_map/reduce_scatter | solution.py:24
  204.5 2.3 multiply_reduce_fusion.1
  206.8 0.0 all-gather.4.cloned.1.call-update
  206.8 0.0 all-reduce.5.cloned.1.call-start
  206.9 60.8 %all-gather.4.cloned.1.call-done = bf16[512,2048]{1,0:T(8,128)(2,1)} async-done(((bf16[32,2048]{1,0:T(8,128)(2,1)}), bf16[512,2048]{1,0:T(8,128)(2,1)}) %all-gather.4.cloned.1.call-update) | async-done | bytes 2097168 | tf_op jit(solution)/shard_map/all_gather | solution.py:34
  267.7 6.5 %fusion.4 = f32[512,1024]{1,0:T(8,128)} fusion(bf16[512,2048]{1,0:T(8,128)(2,1)} %all-gather.4.cloned.1.call-done, bf16[1,1024,2048]{2,1,0:T(8,128)(2,1)} %param.9), kind=kOutput, calls=%fused_computation.6 | convolution fusion | flops 2147483648 | bytes 8388608 | tf_op jit(solution)/shard_map/td,fd->tf/dot_general | solution.py:35
  275.5 39.4 %psum.31 = f32[]{:T(128)} all-reduce(f32[]{:T(128)S(6)} %add.62), channel_id=1, replica_groups=mesh['layer'=2,'latent'=16] {'layer','latent'}, use_global_device_ids=true, to_apply=%region_8.9 | all-reduce | flops 1 | bytes 8 | tf_op jit(solution)/shard_map/psum | solution.py:49
  315.6 6.7 %fusion.10 = bf16[1,1024,2048]{2,1,0:T(8,128)(2,1)} fusion(f32[1024]{0:T(1024)S(1)} %add_sqrt_fusion, bf16[1,1024,2048]{2,1,0:T(8,128)(2,1)} %param.9, f32[1024]{0:T(1024)S(1)} %broadcast_multiply_fusion, bf16[512,2048]{1,0:T(8,128)(2,1)} %all-gather.4.cloned.1.call-done, bf16[512,1024]{1,0:T(8,128)(2,1)S(1)} %get-tuple-element.8), kind=kOutput, calls=%fused_computation.13 | convolution fusion | flops 2157969408 | bytes 11542528 | tf_op jit(solution)/shard_map/tf,td->fd/dot_general | solution.py:44
  322.2 6.5 %convert_bitcast_fusion = bf16[1,2048,1024]{1,2,0:T(8,128)(2,1)} fusion(bf16[1,512,2048]{2,1,0:T(8,128)(2,1)} %all-gather.6.cloned.1.call-done, f32[512,1024]{1,0:T(8,128)} %all-reduce.5.cloned.1.call-done, s32[512,1024]{1,0:T(8,128)S(1)} %copy-done.1, f32[1024]{0:T(1024)S(1)} %broadcast_multiply_fusion.1), kind=kOutput, calls=%fused_computation.12 | convolution fusion | flops 2151677952 | bytes 10489856 | tf_op jit(solution)/shard_map/td,tf->df/dot_general | solution.py:38
  328.8 6.4 %copy.9 = bf16[1,2048,1024]{2,1,0:T(8,128)(2,1)} copy(bf16[1,2048,1024]{1,2,0:T(8,128)(2,1)} %convert_bitcast_fusion) | data formatting | bytes 8388608
  (15 shorter events, 0.1 us)
Async XLA Ops:
  7.2 66.7 %all-gather.6.cloned.1.call-start = ((), (), s32[]{:S(2)}) async-start(), calls=%async_computation.5 | async-start | bytes 2228224 | tf_op jit(solution)/shard_map/all_gather | solution.py:13
  7.9 92.7 %all-reduce.3.cloned.1.call-start = ((), (), s32[]{:S(2)}) async-start(), calls=%async_computation.1 | async-start | bytes 4194304 | tf_op jit(solution)/shard_map/psum | solution.py:17
  80.4 20.3 %copy-start.1 = (s32[512,1024]{1,0:T(8,128)S(1)}, s32[512,1024]{1,0:T(8,128)}, u32[]{:S(2)}) copy-start(s32[512,1024]{1,0:T(8,128)} %param.11) | copy-start | bytes 6291460
  80.4 20.3 %copy-start.4 = (f32[1024]{0:T(1024)S(1)}, f32[1024]{0:T(1024)}, u32[]{:S(2)}) copy-start(f32[1024]{0:T(1024)} %param.8) | copy-start | bytes 12292
  80.4 124.1 %reduce-scatter.2.cloned.1.call-start = ((), (), s32[]{:S(2)}) async-start(), calls=%async_computation.2 | async-start | bytes 4456448 | tf_op jit(solution)/shard_map/reduce_scatter | solution.py:24
  100.6 2.9 copy-start
  107.9 96.6 %copy-start.2 = (bf16[1,32,2048]{2,1,0:T(8,128)(2,1)S(1)}, bf16[1,32,2048]{2,1,0:T(8,128)(2,1)}, u32[]{:S(2)}) copy-start(bf16[1,32,2048]{2,1,0:T(8,128)(2,1)} %param.6) | copy-start | bytes 393220
  107.9 96.6 %copy-start.3 = (f32[1,2048]{1,0:T(1,128)S(1)}, f32[1,2048]{1,0:T(1,128)}, u32[]{:S(2)}) copy-start(f32[1,2048]{1,0:T(1,128)} %param.10) | copy-start | bytes 24580
  108.0 159.7 %all-gather.4.cloned.1.call-start = ((), (), s32[]{:S(2)}) async-start(), calls=%async_computation.3 | async-start | bytes 2228224 | tf_op jit(solution)/shard_map/all_gather | solution.py:34
  206.8 115.4 %all-reduce.5.cloned.1.call-start = ((), (), s32[]{:S(2)}) async-start(), calls=%async_computation.4 | async-start | bytes 4194304 | tf_op jit(solution)/shard_map/psum | solution.py:36
Sparse Core Ops, SparseCore 0:
  10.7 63.0 all-gather.5
  80.5 20.0 all-reduce.2
  108.1 96.3 reduce-scatter.1
  207.7 59.9 all-gather.3
  274.3 20.1 all-reduce.4
where the time goes:
time: 343 us
  waiting for transfers between devices  238 us (69%)
  blocking collectives  41.9 us (12%)
  matrix products  30.6 us (9%)
  between operations  16.9 us (5%)
  other arithmetic  8.39 us (2%)
  local copies, waits for them, and re-layouts  6.41 us (2%)
    reduce_scatter x1, waiting for transfers between devices, per_device(): lax.psum_scatter(jnp.dot(code_b, decoder, preferred_element_type=jnp.floa...  96.5 us
    all_gather x1, waiting for transfers between devices, per_device(): token_all = lax.all_gather(local_rows, 'latent', axis=0, tiled=True)  65.9 us
    all_gather x1, waiting for transfers between devices, per_device(): lax.all_gather(error_share.astype(jnp.bfloat16), 'latent', axis=0, tiled=...  60.8 us
    psum x1, blocking collectives, per_device(): loss_total = lax.psum(square_part + sparse_part, ('layer', 'latent'))  39.4 us
    psum x1, waiting for transfers between devices, per_device(): preact, norm_sum = lax.psum((layer_pre, row_norm), 'layer')  14.5 us
  transfers between devices with their start and end apart: 5, of which 4 were waited for; matrix products, arithmetic and copies ran while one was open for 3% of the time, Pallas kernels for 0%

commit v1 on v0

--- a/solution.py
+++ b/solution.py
@@ -46,7 +46,7 @@
     sparse_part = jnp.where(
         layer_index == 0, sparsity_weight * jnp.sum(latent_code * norm_sum), 0.0
     )
-    loss_total = lax.psum(square_part + sparse_part, ("layer", "latent"))
+    loss_total = lax.psum(lax.psum(square_part + sparse_part, "layer"), "latent")
     loss_value = loss_total / (active_mask.shape[0] * token_all.shape[1])
     return (grad_enc[None], grad_dec[None], loss_value)
 

time: 343 us -> 347 us (1.012)
  blocking collectives: 41.9 us -> 45.7 us
    psum x1 -> x2, blocking collectives: 39.4 us -> 43.2 us  [the longest x1 40.2 us: per_device(): lax.psum(lax.psum(square_part + sparse_part, 'layer'), 'latent')]
where the time goes in v1:
time: 347 us
  waiting for transfers between devices  238 us (69%)
  blocking collectives  45.7 us (13%)
  matrix products  30.5 us (9%)
  between operations  16.9 us (5%)
  other arithmetic  8.42 us (2%)
  local copies, waits for them, and re-layouts  6.41 us (2%)
    reduce_scatter x1, waiting for transfers between devices, per_device(): lax.psum_scatter(jnp.dot(code_b, decoder, preferred_element_type=jnp.floa...  96.6 us
    all_gather x1, waiting for transfers between devices, per_device(): token_all = lax.all_gather(local_rows, 'latent', axis=0, tiled=True)  65.9 us
    all_gather x1, waiting for transfers between devices, per_device(): lax.all_gather(error_share.astype(jnp.bfloat16), 'latent', axis=0, tiled=...  60.8 us
    psum x1, blocking collectives, per_device(): lax.psum(lax.psum(square_part + sparse_part, 'layer'), 'latent')  40.2 us
    psum x1, waiting for transfers between devices, per_device(): preact, norm_sum = lax.psum((layer_pre, row_norm), 'layer')  14.5 us
  transfers between devices with their start and end apart: 5, of which 4 were waited for; matrix products, arithmetic and copies ran while one was open for 3% of the time, Pallas kernels for 0%

profile of v1, /device:TPU:0, one launch (start us, length us, event | category | flops | bytes accessed | tf_op | source)
XLA Modules:
  0.0 346.6 jit_solution(10385726043062331880)
XLA Ops:
  7.2 0.0 all-gather.6.cloned.1.call-start
  7.2 0.7 all-gather.6.cloned.1.call-update
  7.9 0.0 all-reduce.3.cloned.1.call-start
  7.9 65.9 %all-gather.6.cloned.1.call-done = bf16[1,512,2048]{2,1,0:T(8,128)(2,1)} async-done(((bf16[1,32,2048]{2,1,0:T(8,128)(2,1)}), bf16[1,512,2048]{2,1,0:T(8,128)(2,1)}) %all-gather.6.cloned.1.call-update) | async-done | bytes 2097168 | tf_op jit(solution)/shard_map/all_gather | solution.py:13
  73.9 6.5 %fusion.8 = f32[512,1024]{1,0:T(8,128)} fusion(bf16[1,2048,1024]{2,1,0:T(8,128)(2,1)} %param.7, bf16[1,512,2048]{2,1,0:T(8,128)(2,1)} %all-gather.6.cloned.1.call-done), kind=kOutput, calls=%fused_computation.10 | convolution fusion | flops 2147483648 | bytes 8388608 | tf_op jit(solution)/shard_map/dot_general | solution.py:14
  80.3 0.0 all-reduce.3.cloned.1.call-update
  80.4 0.0 reduce-scatter.2.cloned.1.call-start
  80.4 3.2 fusion
  83.7 2.5 psum.37
  86.2 14.5 %all-reduce.3.cloned.1.call-done = f32[512,1024]{1,0:T(8,128)} async-done(((f32[512,1024]{1,0:T(8,128)}), f32[512,1024]{1,0:T(8,128)}) %all-reduce.3.cloned.1.call-update) | async-done | bytes 2097168 | tf_op jit(solution)/shard_map/psum | solution.py:17
  100.6 2.9 multiply_reduce_fusion
  103.6 4.4 %fusion.6 = f32[512,2048]{1,0:T(8,128)} fusion(bf16[1,1024,2048]{2,1,0:T(8,128)(2,1)S(1)} %copy-done, bf16[512,1024]{1,0:T(8,128)(2,1)S(1)} %get-tuple-element.8), kind=kOutput, calls=%fused_computation.8 | convolution fusion | flops 2147483648 | bytes 9437184 | tf_op jit(solution)/shard_map/dot_general | solution.py:25
  108.0 0.0 reduce-scatter.2.cloned.1.call-update
  108.0 0.0 all-gather.4.cloned.1.call-start
  108.0 96.6 %reduce-scatter.2.cloned.1.call-done = f32[32,2048]{1,0:T(8,128)} async-done(((f32[512,2048]{1,0:T(8,128)}), f32[32,2048]{1,0:T(8,128)}) %reduce-scatter.2.cloned.1.call-update) | async-done | bytes 262160 | tf_op jit(solution)/shard_map/reduce_scatter | solution.py:24
  204.6 2.3 multiply_reduce_fusion.1
  206.9 0.0 all-reduce.5.cloned.1.call-start
  206.9 60.8 %all-gather.4.cloned.1.call-done = bf16[512,2048]{1,0:T(8,128)(2,1)} async-done(((bf16[32,2048]{1,0:T(8,128)(2,1)}), bf16[512,2048]{1,0:T(8,128)(2,1)}) %all-gather.4.cloned.1.call-update) | async-done | bytes 2097168 | tf_op jit(solution)/shard_map/all_gather | solution.py:34
  267.7 6.5 %fusion.4 = f32[512,1024]{1,0:T(8,128)} fusion(bf16[512,2048]{1,0:T(8,128)(2,1)} %all-gather.4.cloned.1.call-done, bf16[1,1024,2048]{2,1,0:T(8,128)(2,1)} %param.9), kind=kOutput, calls=%fused_computation.6 | convolution fusion | flops 2147483648 | bytes 8388608 | tf_op jit(solution)/shard_map/td,fd->tf/dot_general | solution.py:35
  275.5 3.0 psum.38
  278.5 40.2 %psum.39 = f32[]{:T(128)} all-reduce(f32[]{:T(128)} %psum.38), channel_id=1, replica_groups=mesh['layer'=2,'latent'=16] {'latent'}, use_global_device_ids=true, to_apply=%region_9.10 | all-reduce | flops 1 | bytes 8 | tf_op jit(solution)/shard_map/psum | solution.py:49
  319.3 6.7 %fusion.10 = bf16[1,1024,2048]{2,1,0:T(8,128)(2,1)} fusion(f32[1024]{0:T(1024)S(1)} %add_sqrt_fusion, bf16[1,1024,2048]{2,1,0:T(8,128)(2,1)} %param.9, f32[1024]{0:T(1024)S(1)} %broadcast_multiply_fusion, bf16[512,2048]{1,0:T(8,128)(2,1)} %all-gather.4.cloned.1.call-done, bf16[512,1024]{1,0:T(8,128)(2,1)S(1)} %get-tuple-element.8), kind=kOutput, calls=%fused_computation.13 | convolution fusion | flops 2157969408 | bytes 11542528 | tf_op jit(solution)/shard_map/tf,td->fd/dot_general | solution.py:44
  326.0 6.5 %convert_bitcast_fusion = bf16[1,2048,1024]{1,2,0:T(8,128)(2,1)} fusion(bf16[1,512,2048]{2,1,0:T(8,128)(2,1)} %all-gather.6.cloned.1.call-done, f32[512,1024]{1,0:T(8,128)} %all-reduce.5.cloned.1.call-done, s32[512,1024]{1,0:T(8,128)S(1)} %copy-done.1, f32[1024]{0:T(1024)S(1)} %broadcast_multiply_fusion.1), kind=kOutput, calls=%fused_computation.12 | convolution fusion | flops 2151677952 | bytes 10489856 | tf_op jit(solution)/shard_map/td,tf->df/dot_general | solution.py:38
  332.6 6.4 %copy.9 = bf16[1,2048,1024]{2,1,0:T(8,128)(2,1)} copy(bf16[1,2048,1024]{1,2,0:T(8,128)(2,1)} %convert_bitcast_fusion) | data formatting | bytes 8388608
  (16 shorter events, 0.1 us)
Async XLA Ops:
  7.2 66.7 %all-gather.6.cloned.1.call-start = ((), (), s32[]{:S(2)}) async-start(), calls=%async_computation.5 | async-start | bytes 2228224 | tf_op jit(solution)/shard_map/all_gather | solution.py:13
  7.9 92.7 %all-reduce.3.cloned.1.call-start = ((), (), s32[]{:S(2)}) async-start(), calls=%async_computation.1 | async-start | bytes 4194304 | tf_op jit(solution)/shard_map/psum | solution.py:17
  80.4 20.3 %copy-start.1 = (s32[512,1024]{1,0:T(8,128)S(1)}, s32[512,1024]{1,0:T(8,128)}, u32[]{:S(2)}) copy-start(s32[512,1024]{1,0:T(8,128)} %param.11) | copy-start | bytes 6291460
  80.4 20.3 %copy-start.4 = (f32[1024]{0:T(1024)S(1)}, f32[1024]{0:T(1024)}, u32[]{:S(2)}) copy-start(f32[1024]{0:T(1024)} %param.8) | copy-start | bytes 12292
  80.4 124.2 %reduce-scatter.2.cloned.1.call-start = ((), (), s32[]{:S(2)}) async-start(), calls=%async_computation.2 | async-start | bytes 4456448 | tf_op jit(solution)/shard_map/reduce_scatter | solution.py:24
  100.6 2.9 copy-start
  107.9 96.6 %copy-start.2 = (bf16[1,32,2048]{2,1,0:T(8,128)(2,1)S(1)}, bf16[1,32,2048]{2,1,0:T(8,128)(2,1)}, u32[]{:S(2)}) copy-start(bf16[1,32,2048]{2,1,0:T(8,128)(2,1)} %param.6) | copy-start | bytes 393220
  108.0 96.6 %copy-start.3 = (f32[1,2048]{1,0:T(1,128)S(1)}, f32[1,2048]{1,0:T(1,128)}, u32[]{:S(2)}) copy-start(f32[1,2048]{1,0:T(1,128)} %param.10) | copy-start | bytes 24580
  108.0 159.7 %all-gather.4.cloned.1.call-start = ((), (), s32[]{:S(2)}) async-start(), calls=%async_computation.3 | async-start | bytes 2228224 | tf_op jit(solution)/shard_map/all_gather | solution.py:34
  206.9 119.1 %all-reduce.5.cloned.1.call-start = ((), (), s32[]{:S(2)}) async-start(), calls=%async_computation.4 | async-start | bytes 4194304 | tf_op jit(solution)/shard_map/psum | solution.py:36
Sparse Core Ops, SparseCore 0:
  10.7 63.0 all-gather.5
  80.5 20.0 all-reduce.2
  108.1 96.4 reduce-scatter.1
  207.8 59.8 all-gather.3
  274.4 20.0 all-reduce.4
